TPU v7x, 128 devices: a whole 4x4x4 slice. The times are simulated.
128 devices in a mesh: row: 16 (over z_lo, y, core), col: 8 (over z_hi, x).
Axes of the slice: x: 4, y: 4, z: 4 (z_hi: 2, z_lo: 2; z = z_hi * 2 + z_lo), core: 2. Of those that a mesh axis runs over, the one named last changes fastest.
Arguments:
- activations: bfloat16 [3072, 16384], P(('row', 'col')), may hold values from -14 to 14
- tenant_ids: int32 [3072], P(('row', 'col')), may hold values from 0 to 63
- concept_labels: int32 [3072], P(('row', 'col')), may hold values from 0 to 1
Outputs:
- covariance: float32 [16384, 16384], P('row', 'col')
- cross: float32 [128, 16384], P(None, ('row', 'col'))
All inputs are finite; a program needn't handle non-finite values.
Results may differ from a plain program's by a relative error of at most 0.0003.
Values may be sent and summed in bfloat16 or wider, within the bound.
A program may use at most 128 MiB of HBM per device.

v0:
```python
import jax
import jax.numpy as jnp
from jax import lax
from jax.sharding import PartitionSpec as P

TENANTS = 64
LABELS = 2


def shards(activations, tenant_ids, concept_labels):
    local_tokens = activations.shape[0]
    width = activations.shape[1]
    row_count = lax.axis_size("row")
    col_count = lax.axis_size("col")
    groups = TENANTS * LABELS
    codes = tenant_ids * LABELS + concept_labels
    codes_rows = lax.all_gather(codes, "row", axis=0, tiled=True)
    row_piece = lax.all_to_all(activations, "row", split_axis=1, concat_axis=0, tiled=True)
    row_panel, codes_all = (
        lax.all_gather(row_piece, "col", axis=0, tiled=True),
        lax.all_gather(codes_rows, "col", axis=0, tiled=True),
    )
    total = row_panel.shape[0]
    row_width = row_panel.shape[1]
    row_view = row_panel.reshape(col_count, row_count, local_tokens, row_width)
    col_piece = lax.all_to_all(activations, "col", split_axis=1, concat_axis=0, tiled=True)
    col_panel = lax.all_gather(col_piece, "row", axis=0, tiled=True)
    col_view = col_panel.reshape(row_count, col_count, local_tokens, col_panel.shape[1])
    gram = jnp.einsum("abtf,batg->fg", row_view, col_view, preferred_element_type=jnp.float32)
    mean_row = jnp.sum(row_panel, axis=0, dtype=jnp.float32) / total
    mean_col = jnp.sum(col_panel, axis=0, dtype=jnp.float32) / total
    covariance = gram / total - mean_row[:, None] * mean_col[None, :]
    slice_width = width // (row_count * col_count)
    slice_start = lax.axis_index("col") * slice_width
    mean_slice = lax.dynamic_slice_in_dim(mean_row, slice_start, slice_width)
    group_ids = jnp.arange(groups, dtype=jnp.int32)
    onehot_all = codes_all[:, None] == group_ids[None, :]
    counts = jnp.sum(onehot_all.astype(jnp.float32), axis=0)
    panel_slice = lax.dynamic_slice_in_dim(row_panel, slice_start, slice_width, 1)
    sums = lax.dot_general(
        onehot_all.astype(jnp.bfloat16),
        panel_slice,
        (((0,), (0,)), ((), ())),
        preferred_element_type=jnp.float32,
    )
    cross = groups / total * (sums - counts[:, None] * mean_slice[None, :])
    return (covariance, cross)


def solution(mesh):
    placed = (P(("row", "col"), None), P(("row", "col")), P(("row", "col")))
    return jax.shard_map(
        shards,
        mesh=mesh,
        in_specs=placed,
        out_specs=(P("row", "col"), P(None, ("row", "col"))),
        check_vma=False,
    )
```

profile of v0, /device:TPU:1, one launch (start us, length us, event | category | flops | bytes accessed | tf_op | source)
XLA Modules:
  0.0 226.1 jit_solution(3943468472371128695)
XLA Ops:
  7.2 0.0 all-gather.4.cloned.1.call-start
  7.2 1.2 copy.29
  8.4 20.0 %all_to_all.38 = bf16[24,16,1024]{2,0,1:T(8,128)(2,1)} all-to-all(bf16[24,16,1024]{2,0,1:T(8,128)(2,1)S(1)} %bitcast.31), channel_id=1, replica_groups=mesh['row'=16,'col'=8] {'row'}, dimensions={1} | all-to-all | bytes 1572864 | tf_op jit(solution)/shard_map/all_to_all | solution.py:18
  28.4 0.0 all-gather.4.cloned.1.call-update
  28.5 0.0 all-gather.6.cloned.1.call-start
  28.5 1.2 copy.28
  29.7 22.4 %all_to_all.39 = bf16[24,8,2048]{2,0,1:T(8,128)(2,1)} all-to-all(bf16[24,8,2048]{2,0,1:T(8,128)(2,1)S(1)} %bitcast.32), channel_id=1, replica_groups=mesh['row'=16,'col'=8] {'col'}, dimensions={1} | all-to-all | bytes 1572864 | tf_op jit(solution)/shard_map/all_to_all | solution.py:26
  52.1 0.0 all-gather.6.cloned.1.call-update
  52.1 1.2 dynamic-slice
  54.0 0.8 add_dynamic-update-slice_fusion
  54.8 10.8 %all-reduce = s32[384]{0:T(512)S(1)} all-reduce(s32[384]{0:T(512)S(1)} %add_dynamic-update-slice_fusion), channel_id=1, replica_groups=mesh['row'=16,'col'=8] {'row'}, use_global_device_ids=true, to_apply=%add | all-reduce | flops 384 | bytes 3072
  65.6 26.1 %all-gather = s32[8,1,384]{2,1,0:T(1,128)S(1)} all-gather(s32[1,1,384]{2,1,0:T(1,128)S(1)} %reshape.30), channel_id=1, replica_groups=mesh['row'=16,'col'=8] {'col'}, dimensions={0}, use_global_device_ids=true | all-gather | bytes 13824 | tf_op jit(solution)/shard_map/all_gather | solution.py:21
  91.7 1.4 convert_reduce_fusion.2
  93.1 28.6 %all-gather.4.cloned.1.call-done = bf16[3072,1024]{1,0:T(8,128)(2,1)} async-done(((bf16[384,1024]{1,0:T(8,128)(2,1)}), bf16[3072,1024]{1,0:T(8,128)(2,1)}) %all-gather.4.cloned.1.call-update) | async-done | bytes 6291472 | tf_op jit(solution)/shard_map/all_gather | solution.py:20
  121.7 3.7 %convert_reduce_fusion.1 = f32[1024]{0:T(1024)S(1)} fusion(bf16[3072,1024]{1,0:T(8,128)(2,1)} %all-gather.4.cloned.1.call-done), kind=kLoop, calls=%fused_computation.3 | loop fusion | flops 6290432 | bytes 6295552 | tf_op jit(solution)/shard_map/reduce_sum | solution.py:30
  125.4 0.1 dynamic_slice.7
  125.5 2.8 %fusion.7 = f32[128,128]{1,0:T(8,128)} fusion(bf16[3072,1024]{1,0:T(8,128)(2,1)} %all-gather.4.cloned.1.call-done, s32[]{:T(128)S(6)} %select_n.4, s32[3072]{0:T(1024)S(1)} %bitcast.34, f32[128]{0:T(128)S(1)} %dynamic_slice.7, f32[128]{0:T(128)S(1)} %convert_reduce_fusion.2), kind=kOutput, calls=%fused_computation.10 | convolution fusion | flops 101105664 | bytes 865284 | tf_op jit(solution)/shard_map/dot_general | solution.py:40
  128.4 65.5 %all-gather.6.cloned.1.call-done = bf16[3072,2048]{1,0:T(8,128)(2,1)} async-done(((bf16[192,2048]{1,0:T(8,128)(2,1)}), bf16[3072,2048]{1,0:T(8,128)(2,1)}) %all-gather.6.cloned.1.call-update) | async-done | bytes 12582928 | tf_op jit(solution)/shard_map/all_gather | solution.py:27
  193.9 6.5 %convert_reduce_fusion = f32[2048]{0:T(1024)S(1)} fusion(bf16[3072,2048]{1,0:T(8,128)(2,1)} %all-gather.6.cloned.1.call-done), kind=kLoop, calls=%fused_computation | loop fusion | flops 12580864 | bytes 12591104 | tf_op jit(solution)/shard_map/reduce_sum | solution.py:31
  200.4 18.9 %fusion.2 = f32[1024,2048]{1,0:T(8,128)} fusion(bf16[8,16,24,1024]{3,2,1,0:T(8,128)(2,1)} %bitcast.26, bf16[16,8,24,2048]{3,2,1,0:T(8,128)(2,1)} %bitcast.25, f32[2048]{0:T(1024)S(1)} %broadcast_multiply_fusion, f32[1024]{0:T(1024)S(1)} %broadcast_multiply_fusion.1), kind=kOutput, calls=%fused_computation.5 | convolution fusion | flops 12891193344 | bytes 27275264 | tf_op jit(solution)/shard_map/abtf,batg->fg/dot_general | solution.py:29
  (4 shorter events, 0.0 us)
Async XLA Ops:
  7.2 114.5 %all-gather.4.cloned.1.call-start = ((), (), s32[]{:S(2)}) async-start(), calls=%async_computation.2 | async-start | bytes 7077888 | tf_op jit(solution)/shard_map/all_gather | solution.py:20
  28.5 165.4 %all-gather.6.cloned.1.call-start = ((), (), s32[]{:S(2)}) async-start(), calls=%async_computation.3 | async-start | bytes 13369344 | tf_op jit(solution)/shard_map/all_gather | solution.py:27
Sparse Core Ops, SparseCore 0:
  28.6 93.0 all-gather.3
  123.4 70.4 all-gather.5
where the time goes:
time: 227 us; the launch traced here: 226 us
  waiting for transfers between devices  94.2 us (41%)
  blocking collectives  79.3 us (35%)
  matrix products  21.8 us (10%)
  between operations  14.7 us (6%)
  other arithmetic  12.3 us (5%)
  local copies, waits for them, and re-layouts  3.72 us (2%)
    all_gather x1, waiting for transfers between devices, shards(): col_panel = lax.all_gather(col_piece, 'row', axis=0, tiled=True)  65.5 us
    all_gather x1, waiting for transfers between devices, shards(): lax.all_gather(row_piece, 'col', axis=0, tiled=True)  28.6 us
    all_gather x1, blocking collectives, shards(): lax.all_gather(codes_rows, 'col', axis=0, tiled=True)  26.1 us
    all_to_all x1, blocking collectives, shards(): lax.all_to_all(activations, 'col', split_axis=1, concat_axis=0, tiled=True)  22.4 us
    all_to_all x1, blocking collectives, shards(): lax.all_to_all(activations, 'row', split_axis=1, concat_axis=0, tiled=True)  20 us
    dot_general x1, matrix products, shards(): jnp.einsum('abtf,batg->fg', row_view, col_view, preferred_element_type=jn...  18.9 us
    unnamed x1, blocking collectives  10.8 us
    reduce_sum x1, other arithmetic, shards(): mean_col = jnp.sum(col_panel, axis=0, dtype=jnp.float32) / total  6.45 us
  transfers between devices with their start and end apart: 2, of which 2 were waited for; matrix products, arithmetic and copies ran while one was open for 5% of the time, Pallas kernels for 0%

commit v1 on v0

--- a/solution.py
+++ b/solution.py
@@ -23,7 +23,12 @@
     total = row_panel.shape[0]
     row_width = row_panel.shape[1]
     row_view = row_panel.reshape(col_count, row_count, local_tokens, row_width)
-    col_piece = lax.all_to_all(activations, "col", split_axis=1, concat_axis=0, tiled=True)
+    col_piece = jnp.concatenate(
+        lax.all_to_all(
+            jnp.stack(jnp.split(activations, lax.axis_size("col"), axis=1)), "col", 0, 0
+        ),
+        axis=0,
+    )
     col_panel = lax.all_gather(col_piece, "row", axis=0, tiled=True)
     col_view = col_panel.reshape(row_count, col_count, local_tokens, col_panel.shape[1])
     gram = jnp.einsum("abtf,batg->fg", row_view, col_view, preferred_element_type=jnp.float32)

time: 227 us -> 240 us (1.057)
  local copies, waits for them, and re-layouts: 3.72 us -> 18.8 us
  waiting for transfers between devices: 94.2 us -> 91.7 us
    unnamed x3 -> x11, local copies, waits for them, and re-layouts: 1.25 us -> 16.7 us
    all_to_all x1, blocking collectives: 22.4 us -> 25 us  [shards(): lax.all_to_all(jnp.stack(jnp.split(activations, lax.axis_size('col'), axi...]
    all_gather x1, waiting for transfers between devices: 28.6 us -> 26.1 us  [shards(): lax.all_gather(row_piece, 'col', axis=0, tiled=True)]
  transfers between devices with their start and end apart: 2 -> 2, of which waited for: 2 -> 2; matrix products, arithmetic and copies ran while one was open for 5% -> 7% of each run, Pallas kernels for 0% -> 0%
where the time goes in v1:
time: 240 us
  waiting for transfers between devices  91.7 us (38%)
  blocking collectives  80.2 us (33%)
  matrix products  21.7 us (9%)
  local copies, waits for them, and re-layouts  18.8 us (8%)
  between operations  14.7 us (6%)
  other arithmetic  12.3 us (5%)
    all_gather x1, waiting for transfers between devices, shards(): col_panel = lax.all_gather(col_piece, 'row', axis=0, tiled=True)  65.5 us
    all_gather x1, waiting for transfers between devices, shards(): lax.all_gather(row_piece, 'col', axis=0, tiled=True)  26.1 us
    all_gather x1, blocking collectives, shards(): lax.all_gather(codes_rows, 'col', axis=0, tiled=True)  26.1 us
    all_to_all x1, blocking collectives, shards(): lax.all_to_all(jnp.stack(jnp.split(activations, lax.axis_size('col'), axi...  25 us
    all_to_all x1, blocking collectives, shards(): lax.all_to_all(activations, 'row', split_axis=1, concat_axis=0, tiled=True)  20 us
    dot_general x1, matrix products, shards(): jnp.einsum('abtf,batg->fg', row_view, col_view, preferred_element_type=jn...  18.8 us
    unnamed x11, local copies, waits for them, and re-layouts  16.7 us
    unnamed x1, blocking collectives  9.1 us
  transfers between devices with their start and end apart: 2, of which 2 were waited for; matrix products, arithmetic and copies ran while one was open for 7% of the time, Pallas kernels for 0%

profile of v1, /device:TPU:1, one launch (start us, length us, event | category | flops | bytes accessed | tf_op | source)
XLA Modules:
  0.0 239.6 jit_solution(7325707023849125161)
XLA Ops:
  7.2 0.0 all-gather.6.cloned.1.call-start
  7.2 1.2 copy.25
  8.4 20.0 %all_to_all.24 = bf16[24,16,1024]{2,0,1:T(8,128)(2,1)} all-to-all(bf16[24,16,1024]{2,0,1:T(8,128)(2,1)S(1)} %bitcast.46), channel_id=1, replica_groups=mesh['row'=16,'col'=8] {'row'}, dimensions={1} | all-to-all | bytes 1572864 | tf_op jit(solution)/shard_map/all_to_all | solution.py:18
  28.4 0.0 all-gather.6.cloned.1.call-update
  28.5 0.0 all-gather.4.cloned.1.call-start
  28.5 0.9 bitcast_dynamic-update-slice_fusion.7
  29.4 0.9 bitcast_dynamic-update-slice_fusion.6
  30.3 0.9 bitcast_dynamic-update-slice_fusion.5
  31.2 0.9 bitcast_dynamic-update-slice_fusion.4
  32.1 0.9 bitcast_dynamic-update-slice_fusion.3
  33.0 0.9 bitcast_dynamic-update-slice_fusion.2
  33.9 0.9 bitcast_dynamic-update-slice_fusion.1
  34.8 0.9 bitcast_dynamic-update-slice_fusion
  35.7 25.0 %all_to_all.25 = bf16[8,24,2048]{2,1,0:T(8,128)(2,1)} all-to-all(bf16[8,24,2048]{2,1,0:T(8,128)(2,1)S(1)} %bitcast_dynamic-update-slice_fusion), channel_id=1, replica_groups=mesh['row'=16,'col'=8] {'col'}, dimensions={0} | all-to-all | bytes 1572864 | tf_op jit(solution)/shard_map/all_to_all | solution.py:27
  60.7 0.0 all-gather.4.cloned.1.call-update
  60.8 1.2 dynamic-slice
  62.7 0.8 add_dynamic-update-slice_fusion
  63.4 9.1 %all-reduce = s32[384]{0:T(512)S(1)} all-reduce(s32[384]{0:T(512)S(1)} %add_dynamic-update-slice_fusion), channel_id=1, replica_groups=mesh['row'=16,'col'=8] {'row'}, use_global_device_ids=true, to_apply=%add | all-reduce | flops 384 | bytes 3072
  72.6 26.1 %all-gather = s32[8,1,384]{2,1,0:T(1,128)S(1)} all-gather(s32[1,1,384]{2,1,0:T(1,128)S(1)} %reshape.31), channel_id=1, replica_groups=mesh['row'=16,'col'=8] {'col'}, dimensions={0}, use_global_device_ids=true | all-gather | bytes 13824 | tf_op jit(solution)/shard_map/all_gather | solution.py:21
  98.6 1.4 convert_reduce_fusion.2
  100.0 26.1 %all-gather.6.cloned.1.call-done = bf16[3072,1024]{1,0:T(8,128)(2,1)} async-done(((bf16[384,1024]{1,0:T(8,128)(2,1)}), bf16[3072,1024]{1,0:T(8,128)(2,1)}) %all-gather.6.cloned.1.call-update) | async-done | bytes 6291472 | tf_op jit(solution)/shard_map/all_gather | solution.py:20
  126.1 3.7 %convert_reduce_fusion.1 = f32[1024]{0:T(1024)S(1)} fusion(bf16[3072,1024]{1,0:T(8,128)(2,1)} %all-gather.6.cloned.1.call-done), kind=kLoop, calls=%fused_computation.3 | loop fusion | flops 6290432 | bytes 6295552 | tf_op jit(solution)/shard_map/reduce_sum | solution.py:35
  129.8 0.1 dynamic_slice.7
  129.9 2.8 %fusion.8 = f32[128,128]{1,0:T(8,128)} fusion(bf16[3072,1024]{1,0:T(8,128)(2,1)} %all-gather.6.cloned.1.call-done, s32[]{:T(128)S(6)} %select_n.4, s32[3072]{0:T(1024)S(1)} %bitcast.48, f32[128]{0:T(128)S(1)} %dynamic_slice.7, f32[128]{0:T(128)S(1)} %convert_reduce_fusion.2), kind=kOutput, calls=%fused_computation.11 | convolution fusion | flops 101105664 | bytes 865284 | tf_op jit(solution)/shard_map/dot_general | solution.py:45
  132.7 65.5 %all-gather.4.cloned.1.call-done = bf16[3072,2048]{1,0:T(8,128)(2,1)} async-done(((bf16[192,2048]{1,0:T(8,128)(2,1)}), bf16[3072,2048]{1,0:T(8,128)(2,1)}) %all-gather.4.cloned.1.call-update) | async-done | bytes 12582928 | tf_op jit(solution)/shard_map/all_gather | solution.py:32
  198.3 6.5 %convert_reduce_fusion = f32[2048]{0:T(1024)S(1)} fusion(bf16[3072,2048]{1,0:T(8,128)(2,1)} %all-gather.4.cloned.1.call-done), kind=kLoop, calls=%fused_computation | loop fusion | flops 12580864 | bytes 12591104 | tf_op jit(solution)/shard_map/reduce_sum | solution.py:36
  204.8 18.8 %fusion.3 = f32[1024,2048]{0,1:T(8,128)} fusion(bf16[8,16,24,1024]{3,2,1,0:T(8,128)(2,1)} %bitcast.42, bf16[16,8,24,2048]{3,2,1,0:T(8,128)(2,1)} %bitcast.41, f32[2048]{0:T(1024)S(1)} %broadcast_multiply_fusion, f32[1024]{0:T(1024)S(1)} %broadcast_multiply_fusion.1), kind=kOutput, calls=%fused_computation.6 | convolution fusion | flops 12891193344 | bytes 27275264 | tf_op jit(solution)/shard_map/abtf,batg->fg/dot_general | solution.py:34
  223.6 9.1 %copy.17 = f32[1024,2048]{1,0:T(8,128)} copy(f32[1024,2048]{0,1:T(8,128)} %fusion.3) | data formatting | bytes 16777216
  (4 shorter events, 0.0 us)
Async XLA Ops:
  7.2 118.9 %all-gather.6.cloned.1.call-start = ((), (), s32[]{:S(2)}) async-start(), calls=%async_computation.3 | async-start | bytes 7077888 | tf_op jit(solution)/shard_map/all_gather | solution.py:20
  28.5 169.8 %all-gather.4.cloned.1.call-start = ((), (), s32[]{:S(2)}) async-start(), calls=%async_computation.2 | async-start | bytes 13369344 | tf_op jit(solution)/shard_map/all_gather | solution.py:32
Sparse Core Ops, SparseCore 0:
  28.6 97.4 all-gather.5
  127.8 70.4 all-gather.3
